TPU v7x, 256 devices: a whole 4x4x8 slice. The times are simulated.
256 devices in a mesh: dp: 32 (over x, y, core), tp: 8 (over z).
Axes of the slice: x: 4, y: 4, z: 8, core: 2. Of those that a mesh axis runs over, the one named last changes fastest.
Arguments:
- arrived_rows: bfloat16 [12288, 7168], P('dp', 'tp'), may hold values from -6 to 6
- row_counts: int32 [32], P('dp'), may hold values from 1 to 384, 4096 in all
- routes: int32 [4096, 8], P('dp'), may hold values from 0 to 31, all different within a row; in each aligned block of 128 rows (0 to 127, 128 to 255, ...) at most 40 rows name the same one
- gate_scale: float32 [4096, 8], P('dp'), may hold values from 0.1 to 0.6
- w_gate: bfloat16 [32, 7168, 1024], P('dp', 'tp'), may hold values from -0.0625 to 0.0625
- w_up: bfloat16 [32, 7168, 1024], P('dp', 'tp'), may hold values from -0.0625 to 0.0625
- w_down: bfloat16 [32, 1024, 7168], P('dp', None, 'tp'), may hold values from -0.1875 to 0.1875
- cotangent: bfloat16 [4096, 7168], P('dp', 'tp'), may hold values from -6 to 6
Outputs:
- layer_out: bfloat16 [4096, 7168], P('dp', 'tp')
- grad_rows: bfloat16 [12288, 7168], P('dp', 'tp')
Inputs may be any that keep to these rules, and one draw needn't show every extreme that they name: `row_counts`: the counts sum to exactly 4096; the largest is exactly 384. `routes`: each row names 8 different experts; within the 128 rows of one index of dp no expert is named by more than 40 rows, a bound that some block reaches.
All inputs are finite; a program needn't handle non-finite values. No bound on the sum of `row_counts` on one device may be relied on, other than what follows from the above.
Results may differ from a plain program's by a relative error of at most 0.03.
Values may be sent and summed in bfloat16 or wider, within the bound.
No kernel may reach another device: no remote copies, remote signals or barrier semaphores. Data moves between devices by JAX's collectives and lax.ppermute only.
A program may use at most 64 MiB of HBM per device.

v0:
```python
import jax
import jax.numpy as jnp
from jax import lax
from jax.sharding import PartitionSpec as P


def rounded(tensor):
    return lax.optimization_barrier(tensor.astype(jnp.bfloat16)).astype(jnp.float32)


def activation_grads(hidden_grad, gate_pre, up_pre):
    sigmoid_gate = jax.nn.sigmoid(gate_pre)
    gate_grad = (
        hidden_grad * up_pre * sigmoid_gate * (1.0 + gate_pre * (1.0 - sigmoid_gate))
    ).astype(jnp.bfloat16)
    up_grad = (hidden_grad * gate_pre * sigmoid_gate).astype(jnp.bfloat16)
    return (gate_grad, up_grad)


def on_device(arrived_rows, row_counts, routes, gate_scale, w_gate, w_up, w_down, cotangent):
    members = lax.axis_size("dp")
    myself = lax.axis_index("dp")
    all_counts = lax.all_gather(row_counts, "dp", axis=0, tiled=True)
    starts = jnp.cumsum(all_counts) - all_counts
    my_start = starts[myself]
    my_count = all_counts[myself]
    slot_count, part_width = arrived_rows.shape
    per_peer = slot_count // members
    row_count, top_count = routes.shape
    capacity = row_count * top_count // members + row_count * top_count // (4 * members)
    target = jnp.arange(members, dtype=jnp.int32)[:, None]
    column = jnp.arange(per_peer, dtype=jnp.int32)[None, :]
    source_slot = (target - my_start) % members + column * members
    outgoing = jnp.where(
        (source_slot < my_count)[:, :, None],
        arrived_rows[jnp.minimum(source_slot, slot_count - 1)],
        0,
    )
    incoming = lax.all_to_all(outgoing, "dp", split_axis=0, concat_axis=0, tiled=True)
    global_rank = jnp.arange(row_count, dtype=jnp.int32) * members + myself
    sender = jnp.sum((starts[None, :] <= global_rank[:, None]).astype(jnp.int32), axis=1) - 1
    offset = global_rank - starts[sender]
    balanced = incoming.reshape(members * per_peer, part_width)[
        sender * per_peer + offset // members
    ]
    expert_ids = routes.reshape(-1)
    pair_total = row_count * top_count
    onehot = (expert_ids[:, None] == jnp.arange(members, dtype=jnp.int32)[None, :]).astype(
        jnp.int32
    )
    earlier = jnp.cumsum(onehot, axis=0) - onehot
    slot_index = jnp.sum(earlier * onehot, axis=1)
    flat_slot = expert_ids * capacity + slot_index
    slot_table = (
        jnp.full((members * capacity,), pair_total, jnp.int32)
        .at[flat_slot]
        .set(jnp.arange(pair_total, dtype=jnp.int32))
    )
    present = slot_table < pair_total
    source_row = jnp.minimum(slot_table, pair_total - 1) // top_count

    def pack_rows(row_block):
        return jnp.where(present[:, None], row_block[source_row], 0).reshape(
            members, capacity, part_width
        )

    def combine_rows(returned):
        picked = returned.reshape(members * capacity, part_width)[flat_slot].reshape(
            row_count, top_count, part_width
        )
        return jnp.einsum("tk,tkd->td", gate_scale, picked.astype(jnp.float32)).astype(jnp.bfloat16)

    gate_proj = w_gate[0]
    up_proj = w_up[0]
    down_proj = w_down[0]
    shipped = lax.all_to_all(pack_rows(balanced), "dp", split_axis=0, concat_axis=0, tiled=True)
    flat_rows = shipped.reshape(-1, part_width)
    gate_part = rounded(jnp.dot(flat_rows, gate_proj, preferred_element_type=jnp.float32))
    up_part = rounded(jnp.dot(flat_rows, up_proj, preferred_element_type=jnp.float32))
    gate_pre = lax.psum(gate_part.astype(jnp.bfloat16), "tp").astype(jnp.float32)
    up_pre = lax.psum(up_part.astype(jnp.bfloat16), "tp").astype(jnp.float32)
    hidden = (jax.nn.silu(gate_pre) * up_pre).astype(jnp.bfloat16)
    expert_out = jnp.dot(hidden, down_proj, preferred_element_type=jnp.float32).astype(jnp.bfloat16)
    expert_out, gate_pre, up_pre = (
        expert_out.reshape(members, capacity, part_width),
        gate_pre,
        up_pre,
    )
    layer_out = combine_rows(
        lax.all_to_all(expert_out, "dp", split_axis=0, concat_axis=0, tiled=True)
    )
    shipped_grad = lax.all_to_all(
        pack_rows(cotangent), "dp", split_axis=0, concat_axis=0, tiled=True
    )
    flat_rows = shipped_grad.reshape(-1, part_width)
    grad_part = rounded(jnp.dot(flat_rows, down_proj.T, preferred_element_type=jnp.float32))
    hidden_grad = lax.psum(grad_part.astype(jnp.bfloat16), "tp").astype(jnp.float32)
    gate_grad, up_grad = activation_grads(hidden_grad, gate_pre, up_pre)
    input_grad = (
        jnp.dot(gate_grad, gate_proj.T, preferred_element_type=jnp.float32)
        + jnp.dot(up_grad, up_proj.T, preferred_element_type=jnp.float32)
    ).astype(jnp.bfloat16)
    input_grad = input_grad.reshape(members, capacity, part_width)
    balanced_grad = combine_rows(
        lax.all_to_all(input_grad, "dp", split_axis=0, concat_axis=0, tiled=True)
    )
    back_rank = starts[:, None] + (myself - starts[:, None]) % members + column * members
    usable = back_rank - starts[:, None] < all_counts[:, None]
    back_pos = jnp.minimum(back_rank // members, row_count - 1)
    leaving = jnp.where(usable[:, :, None], balanced_grad[back_pos], 0)
    arriving = lax.all_to_all(leaving, "dp", split_axis=0, concat_axis=0, tiled=True)
    arrived_index = jnp.arange(slot_count, dtype=jnp.int32)
    from_peer = (my_start + arrived_index) % members
    gathered = arriving.reshape(members * per_peer, part_width)[
        from_peer * per_peer + arrived_index // members
    ]
    grad_rows = jnp.where((arrived_index < my_count)[:, None], gathered, 0)
    return (layer_out, grad_rows)


def solution(mesh):
    placed = (
        P("dp", "tp"),
        P("dp"),
        P("dp", None),
        P("dp", None),
        P("dp", "tp", None),
        P("dp", "tp", None),
        P("dp", None, "tp"),
        P("dp", "tp"),
    )
    return jax.shard_map(
        on_device,
        mesh=mesh,
        in_specs=placed,
        out_specs=(P("dp", "tp"), P("dp", "tp")),
        check_vma=False,
    )
```

profile of v0, /device:TPU:1, one launch (start us, length us, event | category | flops | bytes accessed | tf_op | source)
XLA Modules:
  0.0 451.6 jit_solution(13311008677068077727)
XLA Ops:
  8.0 1.3 dynamic-slice
  9.3 0.8 dynamic-update-slice
  10.0 14.4 %all-reduce = s32[32]{0:T(128)S(1)} all-reduce(s32[32]{0:T(128)S(1)} %dynamic-update-slice), channel_id=1, replica_groups=mesh['dp'=32,'tp'=8] {'dp'}, use_global_device_ids=true, to_apply=%add | all-reduce | flops 32 | bytes 256
  24.7 0.6 dynamic_slice.7
  25.3 0.6 dynamic_slice.6
  25.9 0.7 and_select_fusion.4
  26.7 0.7 subtract_compare_fusion
  27.5 4.0 gather_fusion
  31.5 1.1 reshape.605
  32.6 2.3 broadcast_select_fusion.3
  34.9 7.5 %all-to-all-start = ((bf16[32,12,896]{2,1,0:T(8,128)(2,1)}), bf16[32,12,896]{2,1,0:T(8,128)(2,1)S(1)}, u32[]{:S(2)}, u32[]{:S(2)}) async-start(bf16[32,12,896]{2,1,0:T(8,128)(2,1)} %broadcast_select_fusion.3), calls=%async_computation | async-start | bytes 1835008 | tf_op jit(solution)/shard_map/all_to_all | solution.py:39
  42.9 1.2 gather_fusion.1
  44.1 9.0 %reduce-window.19 = s32[32,8,128]{2,1,0:T(8,128)S(1)} reduce-window(s32[32,8,128]{2,1,0:T(8,128)S(1)} %fusion.28, s32[]{:T(128)} %constant.107.clone.1), window={size=1x1x128 pad=0_0x0_0x127_0}, to_apply=%region_0.0 | reduce-window | flops 4161536 | bytes 262148 | tf_op jit(solution)/shard_map/reduce-window
  53.9 4.3 scatter_custom_fusion
  58.3 5.0 %gather_fusion.5 = bf16[1280,896]{1,0:T(8,128)(2,1)} fusion(bf16[128,896]{1,0:T(8,128)(2,1)S(1)} %copy-done.1, s32[2048]{0:T(1024)S(1)} %pad_clamp_fusion), kind=kCustom, calls=%fused_computation.5 | custom fusion | bytes 4592640 | tf_op jit(solution)/shard_map/gather | solution.py:63
  63.3 0.2 reshape.594
  63.5 0.9 gather_fusion.2
  64.4 5.0 %gather_fusion.3 = bf16[1280,896]{1,0:T(8,128)(2,1)} fusion(bf16[128,896]{1,0:T(8,128)(2,1)S(1)} %gather_fusion.2, s32[2048]{0:T(1024)S(1)} %pad_clamp_fusion), kind=kCustom, calls=%fused_computation.3 | custom fusion | bytes 4592640 | tf_op jit(solution)/shard_map/gather | solution.py:63
  69.4 3.6 broadcast_select_fusion
  73.0 38.2 %all_to_all.30 = bf16[32,40,896]{2,1,0:T(8,128)(2,1)} all-to-all(bf16[32,40,896]{2,1,0:T(8,128)(2,1)S(1)} %get-tuple-element.8), channel_id=1, replica_groups=mesh['dp'=32,'tp'=8] {'dp'}, dimensions={0} | all-to-all | bytes 4587520 | tf_op jit(solution)/shard_map/all_to_all | solution.py:76
  111.2 4.6 %all-to-all-start.3 = ((bf16[32,40,896]{2,1,0:T(8,128)(2,1)}), bf16[32,40,896]{2,1,0:T(8,128)(2,1)}, u32[]{:S(2)}, u32[]{:S(2)}) async-start(bf16[32,40,896]{2,1,0:T(8,128)(2,1)} %get-tuple-element.7), calls=%async_computation.3 | async-start | bytes 4587520 | tf_op jit(solution)/shard_map/all_to_all | solution.py:92
  115.9 0.2 all-reduce.4.cloned.1.call-start
  116.1 6.6 %convolution_convert_fusion.1 = bf16[1280,1024]{1,0:T(8,128)(2,1)} fusion(bf16[1280,896]{1,0:T(8,128)(2,1)} %bitcast.90, bf16[1,896,1024]{2,1,0:T(8,128)(2,1)} %param.13), kind=kOutput, calls=%fused_computation.28 | convolution fusion | flops 2350120960 | bytes 6750208 | tf_op jit(solution)/shard_map/dot_general | solution.py:79
  122.7 23.7 %all-to-all-done.3 = bf16[32,40,896]{2,1,0:T(8,128)(2,1)} async-done(((bf16[32,40,896]{2,1,0:T(8,128)(2,1)}), bf16[32,40,896]{2,1,0:T(8,128)(2,1)}, u32[]{:S(2)}, u32[]{:S(2)}) %all-to-all-start.3) | async-done | bytes 2293792 | tf_op jit(solution)/shard_map/all_to_all | solution.py:92
  146.4 6.8 %convolution_convert_fusion = bf16[1280,1024]{1,0:T(8,128)(2,1)} fusion(bf16[1280,896]{1,0:T(8,128)(2,1)} %bitcast.24, bf16[1,1024,896]{2,1,0:T(8,128)(2,1)} %param.14), kind=kOutput, calls=%fused_computation.27 | convolution fusion | flops 2350120960 | bytes 6750208 | tf_op jit(solution)/shard_map/dot_general | solution.py:96
  153.2 4.1 convolution_convert_fusion.2
  157.4 178.1 %all-reduce.4.cloned.1.call-done = (bf16[1280,1024]{1,0:T(8,128)(2,1)}, bf16[1280,1024]{1,0:T(8,128)(2,1)}, bf16[1280,1024]{1,0:T(8,128)(2,1)}) async-done(((bf16[1280,1024]{1,0:T(8,128)(2,1)}, bf16[1280,1024]{1,0:T(8,128)(2,1)}, bf16[1280,1024]{1,0:T(8,128)(2,1)}), (bf16[1280,1024]{1,0:T(8,128)(2,1)}, bf16[1280,1024]{1,0:T(8,128)(2,1)}, bf16[1280,1024]{1,0:T(8,128)(2,1)})) %all-reduce.4.cloned.1.call-update) | async-done | bytes 7864336 | tf_op jit(solution)/shard_map/psum | solution.py:81
  335.5 7.3 %fusion.13 = f32[1280,896]{1,0:T(8,128)S(1)} fusion(bf16[1280,1024]{1,0:T(8,128)(2,1)} %get-tuple-element.2, bf16[1280,1024]{1,0:T(8,128)(2,1)} %get-tuple-element.4, bf16[1280,1024]{1,0:T(8,128)(2,1)} %get-tuple-element.3, bf16[1,896,1024]{2,1,0:T(8,128)(2,1)S(1)} %copy-done), kind=kOutput, calls=%fused_computation.32 | convolution fusion | flops 2365849600 | bytes 14286848 | tf_op jit(solution)/shard_map/dot_general | solution.py:100
  342.8 4.4 add_convert_fusion
  347.1 7.6 %all-to-all-start.4 = ((bf16[32,40,896]{2,1,0:T(8,128)(2,1)}), bf16[32,40,896]{2,1,0:T(8,128)(2,1)}, u32[]{:S(2)}, u32[]{:S(2)}) async-start(bf16[32,40,896]{2,1,0:T(8,128)(2,1)} %bitcast.92), calls=%async_computation.4 | async-start | bytes 4587520 | tf_op jit(solution)/shard_map/all_to_all | solution.py:105
  354.7 7.7 %convolution_convert_fusion.3 = bf16[1280,896]{1,0:T(8,128)(2,1)} fusion(bf16[1280,1024]{1,0:T(8,128)(2,1)} %get-tuple-element.2, bf16[1280,1024]{1,0:T(8,128)(2,1)} %get-tuple-element.3, bf16[1,1024,896]{2,1,0:T(8,128)(2,1)} %param.14), kind=kOutput, calls=%fused_computation.30 | convolution fusion | flops 2360442880 | bytes 9371648 | tf_op jit(solution)/shard_map/dot_general | solution.py:83
  362.5 22.7 %all-to-all-done.4 = bf16[32,40,896]{2,1,0:T(8,128)(2,1)} async-done(((bf16[32,40,896]{2,1,0:T(8,128)(2,1)}), bf16[32,40,896]{2,1,0:T(8,128)(2,1)}, u32[]{:S(2)}, u32[]{:S(2)}) %all-to-all-start.4) | async-done | bytes 2293792 | tf_op jit(solution)/shard_map/all_to_all | solution.py:105
  385.2 5.5 %all-to-all-start.2 = ((bf16[32,40,896]{2,1,0:T(8,128)(2,1)}), bf16[32,40,896]{2,1,0:T(8,128)(2,1)}, u32[]{:S(2)}, u32[]{:S(2)}) async-start(bf16[32,40,896]{2,1,0:T(8,128)(2,1)} %bitcast.89), calls=%async_computation.2 | async-start | bytes 4587520 | tf_op jit(solution)/shard_map/all_to_all | solution.py:90
  391.0 7.7 %gather_fusion.6 = bf16[1024,896]{1,0:T(8,128)(2,1)} fusion(bf16[1280,896]{1,0:T(8,128)(2,1)} %bitcast.26, s32[1024]{0:T(1024)S(1)} %broadcast_clamp_fusion), kind=kCustom, calls=%fused_computation.6 | custom fusion | bytes 3674112 | tf_op jit(solution)/shard_map/gather | solution.py:68
  398.7 2.2 fusion.15
  401.0 2.3 gather_fusion.7
  403.3 1.1 reshape.661
  404.3 2.3 broadcast_select_fusion.2
  406.6 14.7 %all-to-all-done.2 = bf16[32,40,896]{2,1,0:T(8,128)(2,1)} async-done(((bf16[32,40,896]{2,1,0:T(8,128)(2,1)}), bf16[32,40,896]{2,1,0:T(8,128)(2,1)}, u32[]{:S(2)}, u32[]{:S(2)}) %all-to-all-start.2) | async-done | bytes 2293792 | tf_op jit(solution)/shard_map/all_to_all | solution.py:90
  421.3 4.5 all-to-all-start.5
  425.8 0.7 fusion.39
  426.5 0.7 iota_compare_fusion.2
  427.1 7.7 %gather_fusion.4 = bf16[1024,896]{1,0:T(8,128)(2,1)} fusion(bf16[1280,896]{1,0:T(8,128)(2,1)} %bitcast.19, s32[1024]{0:T(1024)S(1)} %broadcast_clamp_fusion), kind=kCustom, calls=%fused_computation.4 | custom fusion | bytes 3674112 | tf_op jit(solution)/shard_map/gather | solution.py:68
  434.8 2.2 fusion.17
  437.0 0.7 copy.31
  437.8 3.6 all-to-all-done.5
  441.5 2.3 gather_fusion.8
  443.8 1.0 broadcast_select_fusion.4
  (60 shorter events, 2.2 us)
Async XLA Ops:
  7.2 146.1 %copy-start = (bf16[1,896,1024]{2,1,0:T(8,128)(2,1)S(1)}, bf16[1,896,1024]{2,1,0:T(8,128)(2,1)}, u32[]{:S(2)}) copy-start(bf16[1,896,1024]{2,1,0:T(8,128)(2,1)} %param.12) | copy-start | bytes 5505028
  31.5 11.0 %copy-start.3 = (s32[128,8]{0,1:T(8,128)S(1)}, s32[128,8]{0,1:T(8,128)}, u32[]{:S(2)}) copy-start(s32[128,8]{0,1:T(8,128)} %param.10) | copy-start | bytes 12292
  32.6 25.8 %copy-start.1 = (bf16[128,896]{1,0:T(8,128)(2,1)S(1)}, bf16[128,896]{1,0:T(8,128)(2,1)}, u32[]{:S(2)}) copy-start(bf16[128,896]{1,0:T(8,128)(2,1)} %param.15) | copy-start | bytes 688132
  34.9 28.4 %all-to-all-start = ((bf16[32,12,896]{2,1,0:T(8,128)(2,1)}), bf16[32,12,896]{2,1,0:T(8,128)(2,1)S(1)}, u32[]{:S(2)}, u32[]{:S(2)}) async-start(bf16[32,12,896]{2,1,0:T(8,128)(2,1)} %broadcast_select_fusion.3), calls=%async_computation | async-start | bytes 1835008 | tf_op jit(solution)/shard_map/all_to_all | solution.py:39
  111.2 35.2 %all-to-all-start.3 = ((bf16[32,40,896]{2,1,0:T(8,128)(2,1)}), bf16[32,40,896]{2,1,0:T(8,128)(2,1)}, u32[]{:S(2)}, u32[]{:S(2)}) async-start(bf16[32,40,896]{2,1,0:T(8,128)(2,1)} %get-tuple-element.7), calls=%async_computation.3 | async-start | bytes 4587520 | tf_op jit(solution)/shard_map/all_to_all | solution.py:92
  115.9 219.6 %all-reduce.4.cloned.1.call-start = ((), (), s32[]{:S(2)}) async-start(), calls=%async_computation.6 | async-start | bytes 15728640 | tf_op jit(solution)/shard_map/psum | solution.py:81
  146.4 6.8 %copy-start.2 = (bf16[32,40,896]{2,1,0:T(8,128)(2,1)S(1)}, bf16[32,40,896]{2,1,0:T(8,128)(2,1)}, u32[]{:S(2)}) copy-start(bf16[32,40,896]{2,1,0:T(8,128)(2,1)} %all_to_all.30) | copy-start | bytes 6881284
  335.5 7.3 %copy-start.5 = (bf16[1280,1024]{1,0:T(8,128)(2,1)S(1)}, bf16[1280,1024]{1,0:T(8,128)(2,1)}, u32[]{:S(2)}) copy-start(bf16[1280,1024]{1,0:T(8,128)(2,1)} %get-tuple-element.3) | copy-start | bytes 7864324
  335.5 7.3 %copy-start.6 = (bf16[1280,1024]{1,0:T(8,128)(2,1)S(1)}, bf16[1280,1024]{1,0:T(8,128)(2,1)}, u32[]{:S(2)}) copy-start(bf16[1280,1024]{1,0:T(8,128)(2,1)} %get-tuple-element.4) | copy-start | bytes 7864324
  335.5 7.3 %copy-start.7 = (bf16[1,896,1024]{2,1,0:T(8,128)(2,1)S(1)}, bf16[1,896,1024]{2,1,0:T(8,128)(2,1)}, u32[]{:S(2)}) copy-start(bf16[1,896,1024]{2,1,0:T(8,128)(2,1)} %param.13) | copy-start | bytes 5505028
  347.1 38.1 %all-to-all-start.4 = ((bf16[32,40,896]{2,1,0:T(8,128)(2,1)}), bf16[32,40,896]{2,1,0:T(8,128)(2,1)}, u32[]{:S(2)}, u32[]{:S(2)}) async-start(bf16[32,40,896]{2,1,0:T(8,128)(2,1)} %bitcast.92), calls=%async_computation.4 | async-start | bytes 4587520 | tf_op jit(solution)/shard_map/all_to_all | solution.py:105
  362.5 28.2 %copy-start.4 = (f32[128,8]{0,1:T(8,128)S(1)}, f32[128,8]{0,1:T(8,128)}, u32[]{:S(2)}) copy-start(f32[128,8]{0,1:T(8,128)} %param.11) | copy-start | bytes 12292
  385.2 36.1 %all-to-all-start.2 = ((bf16[32,40,896]{2,1,0:T(8,128)(2,1)}), bf16[32,40,896]{2,1,0:T(8,128)(2,1)}, u32[]{:S(2)}, u32[]{:S(2)}) async-start(bf16[32,40,896]{2,1,0:T(8,128)(2,1)} %bitcast.89), calls=%async_computation.2 | async-start | bytes 4587520 | tf_op jit(solution)/shard_map/all_to_all | solution.py:90
  421.3 20.1 %all-to-all-start.5 = ((bf16[32,12,896]{2,1,0:T(8,128)(2,1)}), bf16[32,12,896]{2,1,0:T(8,128)(2,1)S(1)}, u32[]{:S(2)}, u32[]{:S(2)}) async-start(bf16[32,12,896]{2,1,0:T(8,128)(2,1)} %broadcast_select_fusion.2), calls=%async_computation.5 | async-start | bytes 1835008 | tf_op jit(solution)/shard_map/all_to_all | solution.py:111
Sparse Core Ops, SparseCore 0:
  157.5 177.9 all-reduce.3
where the time goes:
time: 453 us; the launch traced here: 452 us
  waiting for transfers between devices  243 us (54%)
  blocking collectives  52.6 us (12%)
  local copies, waits for them, and re-layouts  48.1 us (11%)
  matrix products  41.3 us (9%)
  starting transfers between devices  30 us (7%)
  other arithmetic  21.6 us (5%)
  between operations  15.2 us (3%)
    psum x1, waiting for transfers between devices, on_device(): up_pre = lax.psum(up_part.astype(jnp.bfloat16), 'tp').astype(jnp.float32)  178 us
    all_to_all x1, blocking collectives, on_device(): lax.all_to_all(pack_rows(balanced), 'dp', split_axis=0, concat_axis=0, ti...  38.2 us
    all_to_all x1, waiting for transfers between devices, on_device(): lax.all_to_all(pack_rows(cotangent), 'dp', split_axis=0, concat_axis=0, t...  23.7 us
    all_to_all x1, waiting for transfers between devices, on_device(): lax.all_to_all(input_grad, 'dp', split_axis=0, concat_axis=0, tiled=True)  22.7 us
    gather x2, local copies, waits for them, and re-layouts, combine_rows(): returned.reshape(members * capacity, part_width)[flat_slot]  15.4 us
    all_to_all x1, waiting for transfers between devices, on_device(): lax.all_to_all(expert_out, 'dp', split_axis=0, concat_axis=0, tiled=True)  14.7 us
    unnamed x1, blocking collectives  14.4 us
    gather x2, local copies, waits for them, and re-layouts, pack_rows(): row_block[source_row]  9.98 us
  transfers between devices with their start and end apart: 6, of which 5 were waited for; matrix products, arithmetic and copies ran while one was open for 14% of the time, Pallas kernels for 0%

commit v1 on v0

--- a/solution.py
+++ b/solution.py
@@ -78,7 +78,7 @@
     gate_part = rounded(jnp.dot(flat_rows, gate_proj, preferred_element_type=jnp.float32))
     up_part = rounded(jnp.dot(flat_rows, up_proj, preferred_element_type=jnp.float32))
     gate_pre = lax.psum(gate_part.astype(jnp.bfloat16), "tp").astype(jnp.float32)
-    up_pre = lax.psum(up_part.astype(jnp.bfloat16), "tp").astype(jnp.float32)
+    up_pre = jnp.sum(lax.all_gather(up_part.astype(jnp.bfloat16), "tp"), axis=0).astype(jnp.float32)
     hidden = (jax.nn.silu(gate_pre) * up_pre).astype(jnp.bfloat16)
     expert_out = jnp.dot(hidden, down_proj, preferred_element_type=jnp.float32).astype(jnp.bfloat16)
     expert_out, gate_pre, up_pre = (

time: 453 us -> 577 us (1.27)
  waiting for transfers between devices: 243 us -> 355 us
  other arithmetic: 21.6 us -> 34.9 us
    all_gather x0 -> x1, waiting for transfers between devices: none -> 169 us  [on_device(): lax.all_gather(up_part.astype(jnp.bfloat16), 'tp')]
    psum x1, waiting for transfers between devices: 178 us -> 117 us  [on_device(): lax.psum(gate_part.astype(jnp.bfloat16), 'tp').astype(jnp.float32)]
    reduce_sum x0 -> x1, other arithmetic: none -> 13.2 us  [on_device(): jnp.sum(lax.all_gather(up_part.astype(jnp.bfloat16), 'tp'), axis=0)]
  transfers between devices with their start and end apart: 6 -> 7, of which waited for: 5 -> 6; matrix products, arithmetic and copies ran while one was open for 14% -> 14% of each run, Pallas kernels for 0% -> 0%
where the time goes in v1:
time: 577 us; the launch traced here: 576 us
  waiting for transfers between devices  355 us (62%)
  blocking collectives  52.7 us (9%)
  local copies, waits for them, and re-layouts  48.2 us (8%)
  matrix products  39.7 us (7%)
  other arithmetic  34.9 us (6%)
  starting transfers between devices  30.1 us (5%)
  between operations  15.3 us (3%)
    all_gather x1, waiting for transfers between devices, on_device(): lax.all_gather(up_part.astype(jnp.bfloat16), 'tp')  169 us
    psum x1, waiting for transfers between devices, on_device(): lax.psum(gate_part.astype(jnp.bfloat16), 'tp').astype(jnp.float32)  117 us
    all_to_all x1, blocking collectives, on_device(): lax.all_to_all(pack_rows(balanced), 'dp', split_axis=0, concat_axis=0, ti...  38.2 us
    all_to_all x1, waiting for transfers between devices, on_device(): lax.all_to_all(pack_rows(cotangent), 'dp', split_axis=0, concat_axis=0, t...  24.4 us
    all_to_all x1, waiting for transfers between devices, on_device(): lax.all_to_all(input_grad, 'dp', split_axis=0, concat_axis=0, tiled=True)  23.5 us
    all_to_all x1, waiting for transfers between devices, on_device(): lax.all_to_all(expert_out, 'dp', split_axis=0, concat_axis=0, tiled=True)  14.6 us
    unnamed x1, blocking collectives  14.4 us
    reduce_sum x1, other arithmetic, on_device(): jnp.sum(lax.all_gather(up_part.astype(jnp.bfloat16), 'tp'), axis=0)  13.2 us
  transfers between devices with their start and end apart: 7, of which 6 were waited for; matrix products, arithmetic and copies ran while one was open for 14% of the time, Pallas kernels for 0%

profile of v1, /device:TPU:1, one launch (start us, length us, event | category | flops | bytes accessed | tf_op | source)
XLA Modules:
  0.0 575.6 jit_solution(9092956024850269712)
XLA Ops:
  8.0 1.3 dynamic-slice
  9.3 0.8 dynamic-update-slice
  10.0 14.4 %all-reduce = s32[32]{0:T(128)S(1)} all-reduce(s32[32]{0:T(128)S(1)} %dynamic-update-slice), channel_id=1, replica_groups=mesh['dp'=32,'tp'=8] {'dp'}, use_global_device_ids=true, to_apply=%add | all-reduce | flops 32 | bytes 256
  25.9 0.7 and_select_fusion.4
  26.8 4.0 gather_fusion
  30.7 1.1 reshape.605
  31.8 0.7 subtract_compare_fusion
  32.6 2.3 broadcast_select_fusion.3
  34.9 8.2 %all-to-all-start = ((bf16[32,12,896]{2,1,0:T(8,128)(2,1)}), bf16[32,12,896]{2,1,0:T(8,128)(2,1)}, u32[]{:S(2)}, u32[]{:S(2)}) async-start(bf16[32,12,896]{2,1,0:T(8,128)(2,1)} %broadcast_select_fusion.3), calls=%async_computation | async-start | bytes 1835008 | tf_op jit(solution)/shard_map/all_to_all | solution.py:39
  43.7 9.0 %reduce-window.19 = s32[32,8,128]{2,1,0:T(8,128)S(1)} reduce-window(s32[32,8,128]{2,1,0:T(8,128)S(1)} %fusion.28, s32[]{:T(128)} %constant.109.clone.1), window={size=1x1x128 pad=0_0x0_0x127_0}, to_apply=%region_0.0 | reduce-window | flops 4161536 | bytes 262148 | tf_op jit(solution)/shard_map/reduce-window
  53.3 4.3 scatter_custom_fusion
  57.8 1.2 gather_fusion.1
  59.1 5.0 gather_fusion.5
  64.1 1.3 reshape.594
  65.4 0.9 gather_fusion.2
  66.3 4.9 gather_fusion.3
  71.2 3.6 broadcast_select_fusion
  74.8 38.2 %all_to_all.30 = bf16[32,40,896]{2,1,0:T(8,128)(2,1)S(1)} all-to-all(bf16[32,40,896]{2,1,0:T(8,128)(2,1)S(1)} %get-tuple-element.7), channel_id=1, replica_groups=mesh['dp'=32,'tp'=8] {'dp'}, dimensions={0} | all-to-all | bytes 4587520 | tf_op jit(solution)/shard_map/all_to_all | solution.py:76
  113.1 1.4 copy-done.4
  114.5 4.2 convolution_convert_fusion.1
  118.7 4.6 all-to-all-start.3
  123.6 5.9 %convolution_convert_fusion.2 = bf16[1280,1024]{1,0:T(8,128)(2,1)} fusion(bf16[1280,896]{1,0:T(8,128)(2,1)} %bitcast.94, bf16[1,896,1024]{2,1,0:T(8,128)(2,1)S(1)} %copy-done), kind=kOutput, calls=%fused_computation.29 | convolution fusion | flops 2350120960 | bytes 6750208 | tf_op jit(solution)/shard_map/dot_general | solution.py:78
  129.5 24.4 %all-to-all-done.3 = bf16[32,40,896]{2,1,0:T(8,128)(2,1)} async-done(((bf16[32,40,896]{2,1,0:T(8,128)(2,1)}), bf16[32,40,896]{2,1,0:T(8,128)(2,1)}, u32[]{:S(2)}, u32[]{:S(2)}) %all-to-all-start.3) | async-done | bytes 2293792 | tf_op jit(solution)/shard_map/all_to_all | solution.py:92
  153.9 6.7 %convolution_convert_fusion = bf16[1280,1024]{1,0:T(8,128)(2,1)} fusion(bf16[1280,896]{1,0:T(8,128)(2,1)} %bitcast.25, bf16[1,1024,896]{2,1,0:T(8,128)(2,1)} %param.14), kind=kOutput, calls=%fused_computation.27 | convolution fusion | flops 2350120960 | bytes 6750208 | tf_op jit(solution)/shard_map/dot_general | solution.py:96
  160.6 169.2 %all-gather.3.cloned.1.call-done = bf16[10240,1024]{1,0:T(8,128)(2,1)} async-done(((bf16[1280,1024]{1,0:T(8,128)(2,1)}), bf16[10240,1024]{1,0:T(8,128)(2,1)}) %all-gather.3.cloned.1.call-update) | async-done | bytes 20971536 | tf_op jit(solution)/shard_map/all_gather | solution.py:81
  329.9 13.2 %reduce_sum.35 = bf16[1280,1024]{1,0:T(8,128)(2,1)} reduce(bf16[8,1280,1024]{2,1,0:T(8,128)(2,1)} %bitcast.89, bf16[]{:T(256)} %constant.117.clone.1), dimensions={0}, to_apply=%region_7.8 | reduce | flops 9175040 | bytes 23592962 | tf_op jit(solution)/shard_map/reduce_sum | solution.py:81
  343.1 117.0 %all-reduce.4.cloned.1.call-done = (bf16[1280,1024]{1,0:T(8,128)(2,1)}, bf16[1280,1024]{1,0:T(8,128)(2,1)}) async-done(((bf16[1280,1024]{1,0:T(8,128)(2,1)}, bf16[1280,1024]{1,0:T(8,128)(2,1)}), (bf16[1280,1024]{1,0:T(8,128)(2,1)}, bf16[1280,1024]{1,0:T(8,128)(2,1)})) %all-reduce.4.cloned.1.call-update) | async-done | bytes 5242896 | tf_op jit(solution)/shard_map/psum | solution.py:80
  460.1 7.3 %fusion.13 = f32[1280,896]{1,0:T(8,128)S(1)} fusion(bf16[1280,1024]{1,0:T(8,128)(2,1)} %reduce_sum.35, bf16[1280,1024]{1,0:T(8,128)(2,1)} %get-tuple-element.3, bf16[1280,1024]{1,0:T(8,128)(2,1)} %get-tuple-element.2, bf16[1,896,1024]{2,1,0:T(8,128)(2,1)S(1)} %copy-done), kind=kOutput, calls=%fused_computation.32 | convolution fusion | flops 2365849600 | bytes 14286848 | tf_op jit(solution)/shard_map/dot_general | solution.py:100
  467.4 4.4 add_convert_fusion
  471.8 7.9 %all-to-all-start.4 = ((bf16[32,40,896]{2,1,0:T(8,128)(2,1)}), bf16[32,40,896]{2,1,0:T(8,128)(2,1)}, u32[]{:S(2)}, u32[]{:S(2)}) async-start(bf16[32,40,896]{2,1,0:T(8,128)(2,1)} %bitcast.95), calls=%async_computation.4 | async-start | bytes 4587520 | tf_op jit(solution)/shard_map/all_to_all | solution.py:105
  479.7 6.9 %convolution_convert_fusion.3 = bf16[1280,896]{1,0:T(8,128)(2,1)} fusion(bf16[1280,1024]{1,0:T(8,128)(2,1)S(1)} %copy-done.3, bf16[1280,1024]{1,0:T(8,128)(2,1)} %get-tuple-element.2, bf16[1,1024,896]{2,1,0:T(8,128)(2,1)} %param.14), kind=kOutput, calls=%fused_computation.30 | convolution fusion | flops 2360442880 | bytes 9371648 | tf_op jit(solution)/shard_map/dot_general | solution.py:83
  486.6 23.5 %all-to-all-done.4 = bf16[32,40,896]{2,1,0:T(8,128)(2,1)} async-done(((bf16[32,40,896]{2,1,0:T(8,128)(2,1)}), bf16[32,40,896]{2,1,0:T(8,128)(2,1)}, u32[]{:S(2)}, u32[]{:S(2)}) %all-to-all-start.4) | async-done | bytes 2293792 | tf_op jit(solution)/shard_map/all_to_all | solution.py:105
  510.1 4.6 all-to-all-start.2
  515.0 7.7 %gather_fusion.6 = bf16[1024,896]{1,0:T(8,128)(2,1)} fusion(bf16[1280,896]{1,0:T(8,128)(2,1)} %bitcast.27, s32[1024]{0:T(1024)S(1)} %broadcast_clamp_fusion), kind=kCustom, calls=%fused_computation.6 | custom fusion | bytes 3674112 | tf_op jit(solution)/shard_map/gather | solution.py:68
  522.8 2.2 fusion.15
  525.0 2.3 gather_fusion.7
  527.3 1.1 reshape.661
  528.4 2.3 broadcast_select_fusion.2
  530.7 14.6 %all-to-all-done.2 = bf16[32,40,896]{2,1,0:T(8,128)(2,1)S(1)} async-done(((bf16[32,40,896]{2,1,0:T(8,128)(2,1)}), bf16[32,40,896]{2,1,0:T(8,128)(2,1)S(1)}, u32[]{:S(2)}, u32[]{:S(2)}) %all-to-all-start.2) | async-done | bytes 2293792 | tf_op jit(solution)/shard_map/all_to_all | solution.py:90
  545.2 4.5 all-to-all-start.5
  549.7 0.7 fusion.39
  550.4 0.7 iota_compare_fusion.2
  551.1 5.2 gather_fusion.4
  556.3 2.2 fusion.17
  558.5 0.7 copy.31
  559.2 6.1 %all-to-all-done.5 = bf16[32,12,896]{2,1,0:T(8,128)(2,1)S(1)} async-done(((bf16[32,12,896]{2,1,0:T(8,128)(2,1)}), bf16[32,12,896]{2,1,0:T(8,128)(2,1)S(1)}, u32[]{:S(2)}, u32[]{:S(2)}) %all-to-all-start.5) | async-done | bytes 688160 | tf_op jit(solution)/shard_map/all_to_all | solution.py:111
  565.5 2.3 gather_fusion.8
  567.8 1.0 broadcast_select_fusion.4
  (70 shorter events, 3.7 us)
Async XLA Ops:
  7.2 116.4 %copy-start = (bf16[1,896,1024]{2,1,0:T(8,128)(2,1)S(1)}, bf16[1,896,1024]{2,1,0:T(8,128)(2,1)}, u32[]{:S(2)}) copy-start(bf16[1,896,1024]{2,1,0:T(8,128)(2,1)} %param.12) | copy-start | bytes 5505028
  30.7 12.4 %copy-start.5 = (s32[128,8]{0,1:T(8,128)S(1)}, s32[128,8]{0,1:T(8,128)}, u32[]{:S(2)}) copy-start(s32[128,8]{0,1:T(8,128)} %param.10) | copy-start | bytes 12292
  32.6 26.5 %copy-start.2 = (bf16[128,896]{1,0:T(8,128)(2,1)S(1)}, bf16[128,896]{1,0:T(8,128)(2,1)}, u32[]{:S(2)}) copy-start(bf16[128,896]{1,0:T(8,128)(2,1)} %param.15) | copy-start | bytes 688132
  34.9 29.1 %all-to-all-start = ((bf16[32,12,896]{2,1,0:T(8,128)(2,1)}), bf16[32,12,896]{2,1,0:T(8,128)(2,1)}, u32[]{:S(2)}, u32[]{:S(2)}) async-start(bf16[32,12,896]{2,1,0:T(8,128)(2,1)} %broadcast_select_fusion.3), calls=%async_computation | async-start | bytes 1835008 | tf_op jit(solution)/shard_map/all_to_all | solution.py:39
  43.1 286.7 %all-gather.3.cloned.1.call-start = ((), (), s32[]{:S(2)}) async-start(), calls=%async_computation.6 | async-start | bytes 23592960 | tf_op jit(solution)/shard_map/all_gather | solution.py:81
  74.8 39.6 %copy-start.9 = (bf16[1,896,1024]{2,1,0:T(8,128)(2,1)S(1)}, bf16[1,896,1024]{2,1,0:T(8,128)(2,1)}, u32[]{:S(2)}) copy-start(bf16[1,896,1024]{2,1,0:T(8,128)(2,1)} %param.13) | copy-start | bytes 5505028
  113.0 1.4 copy-start.4
  118.7 35.2 %all-to-all-start.3 = ((bf16[32,40,896]{2,1,0:T(8,128)(2,1)}), bf16[32,40,896]{2,1,0:T(8,128)(2,1)}, u32[]{:S(2)}, u32[]{:S(2)}) async-start(bf16[32,40,896]{2,1,0:T(8,128)(2,1)} %get-tuple-element.6), calls=%async_computation.3 | async-start | bytes 4587520 | tf_op jit(solution)/shard_map/all_to_all | solution.py:92
  123.4 336.7 %all-reduce.4.cloned.1.call-start = ((), (), s32[]{:S(2)}) async-start(), calls=%async_computation.7 | async-start | bytes 10485760 | tf_op jit(solution)/shard_map/psum | solution.py:80
  460.1 7.3 %copy-start.7 = (bf16[1280,1024]{1,0:T(8,128)(2,1)S(1)}, bf16[1280,1024]{1,0:T(8,128)(2,1)}, u32[]{:S(2)}) copy-start(bf16[1280,1024]{1,0:T(8,128)(2,1)} %get-tuple-element.2) | copy-start | bytes 7864324
  460.1 7.3 %copy-start.8 = (bf16[1280,1024]{1,0:T(8,128)(2,1)S(1)}, bf16[1280,1024]{1,0:T(8,128)(2,1)}, u32[]{:S(2)}) copy-start(bf16[1280,1024]{1,0:T(8,128)(2,1)} %get-tuple-element.3) | copy-start | bytes 7864324
  460.1 7.3 %copy-start.10 = (bf16[1,896,1024]{2,1,0:T(8,128)(2,1)S(1)}, bf16[1,896,1024]{2,1,0:T(8,128)(2,1)}, u32[]{:S(2)}) copy-start(bf16[1,896,1024]{2,1,0:T(8,128)(2,1)} %param.13) | copy-start | bytes 5505028
  471.8 7.9 %copy-start.3 = (bf16[1280,1024]{1,0:T(8,128)(2,1)S(1)}, bf16[1280,1024]{1,0:T(8,128)(2,1)}, u32[]{:S(2)}) copy-start(bf16[1280,1024]{1,0:T(8,128)(2,1)} %reduce_sum.35) | copy-start | bytes 7864324
  471.8 38.3 %all-to-all-start.4 = ((bf16[32,40,896]{2,1,0:T(8,128)(2,1)}), bf16[32,40,896]{2,1,0:T(8,128)(2,1)}, u32[]{:S(2)}, u32[]{:S(2)}) async-start(bf16[32,40,896]{2,1,0:T(8,128)(2,1)} %bitcast.95), calls=%async_computation.4 | async-start | bytes 4587520 | tf_op jit(solution)/shard_map/all_to_all | solution.py:105
  486.6 28.2 %copy-start.6 = (f32[128,8]{0,1:T(8,128)S(1)}, f32[128,8]{0,1:T(8,128)}, u32[]{:S(2)}) copy-start(f32[128,8]{0,1:T(8,128)} %param.11) | copy-start | bytes 12292
  510.1 35.1 %all-to-all-start.2 = ((bf16[32,40,896]{2,1,0:T(8,128)(2,1)}), bf16[32,40,896]{2,1,0:T(8,128)(2,1)S(1)}, u32[]{:S(2)}, u32[]{:S(2)}) async-start(bf16[32,40,896]{2,1,0:T(8,128)(2,1)} %bitcast.92), calls=%async_computation.2 | async-start | bytes 4587520 | tf_op jit(solution)/shard_map/all_to_all | solution.py:90
  545.2 20.1 %all-to-all-start.5 = ((bf16[32,12,896]{2,1,0:T(8,128)(2,1)}), bf16[32,12,896]{2,1,0:T(8,128)(2,1)S(1)}, u32[]{:S(2)}, u32[]{:S(2)}) async-start(bf16[32,12,896]{2,1,0:T(8,128)(2,1)} %broadcast_select_fusion.2), calls=%async_computation.5 | async-start | bytes 1835008 | tf_op jit(solution)/shard_map/all_to_all | solution.py:111
  565.3 3.5 copy-start.1
Sparse Core Ops, SparseCore 0:
  118.8 211.0 all-gather.2
  332.3 127.7 all-reduce.3
